TPU v7x, 32 devices: a whole 2x2x4 slice. The times are simulated.
32 devices in a mesh: comp: 4 (over y, x), dom: 8 (over z, core).
Axes of the slice: x: 2, y: 2, z: 4, core: 2. Of those that a mesh axis runs over, the one named last changes fastest.
Arguments:
- state: float32 [72, 524288], P(None, ('comp', 'dom')), may hold values from -6 to 6
- forcing: float32 [8, 524288], P(None, ('comp', 'dom')), may hold values from -6 to 6
- vertical: float32 [4, 72, 72], P('comp'), may hold values from -0.75 to 0.75
- inject: float32 [4, 72, 8], P('comp'), may hold values from -2 to 2
- extract: float32 [4, 8, 72], P('comp'), may hold values from -0.75 to 0.75
- diffuse: float32 [524288], P(('comp', 'dom')), may hold values from 0.05 to 0.24
- substeps: int32 [524288], P(('comp', 'dom')), may hold values from 1 to 4, as said below
- landmask: int32 [524288], P(('comp', 'dom')), may hold values 0 or 1
- links: int32 [3, 32, 32, 2], P(None, ('comp', 'dom')), may hold values from -1 to 127, as said below
- remap_weight_matrices: float32 [512, 128, 128], P(('comp', 'dom')), may hold values from -0.5 to 0.5
Outputs:
- state_next: float32 [72, 524288], P(None, ('comp', 'dom'))
- forcing_next: float32 [8, 524288], P(None, ('comp', 'dom'))
Inputs may be any that keep to these rules, and one draw needn't show every extreme that they name: substeps holds each column's count of substeps; 4 and 1 occur in every draw. In each [g, h, k] either all three fields are -1 (an empty slot) or links[0] and links[1] are blocks 0 to 127 and links[2] a slot 0 to 15; live slots of a pair come first; live entries join an atmosphere device (index below (3) * 8) with an ocean device only, and every such pair has one or more live slots; a pair has at most 2 live slots, and some pair reaches 2 in every draw.
All inputs are finite; a program needn't handle non-finite values. No bound on the sum of `landmask` on one device may be relied on, other than what follows from the above.
Results may differ from a plain program's by a relative error of at most 0.0003.
Values sent between devices are 32-bit elements; how exact they have to be, the bound alone decides.
A program may use at most 128 MiB of HBM per device.

v0:
```python
import jax
import jax.numpy as jnp
from jax import lax
from jax.sharding import PartitionSpec as P

SUBS = 4


DT = 0.25


def with_halo(cells, sides, width):
    for axis, dim in sides:
        count = lax.axis_size(axis)
        head = lax.slice_in_dim(cells, 0, width, axis=dim)
        tail = lax.slice_in_dim(cells, cells.shape[dim] - width, cells.shape[dim], axis=dim)
        cells = jnp.concatenate(
            [
                lax.ppermute(tail, axis, [(i, (i + 1) % count) for i in range(count)]),
                cells,
                lax.ppermute(head, axis, [((i + 1) % count, i) for i in range(count)]),
            ],
            axis=dim,
        )
    return cells


def local(
    state,
    forcing,
    vertical,
    inject,
    extract,
    diffuse,
    substeps,
    landmask,
    links,
    remap_weight_matrices,
):
    highest = lax.Precision.HIGHEST
    fields = forcing.shape[0]
    columns = state.shape[1]
    block_width = remap_weight_matrices.shape[1]
    block_count = columns // block_width
    wet_cells = landmask.astype(jnp.float32)
    coupled = (
        jnp.dot(extract[0], state, precision=highest, preferred_element_type=jnp.float32)
        * wet_cells
    )
    blocks = coupled.reshape(fields, block_count, block_width).transpose(1, 0, 2)
    device_link_table = links[:, 0]
    peer_count = device_link_table.shape[1]
    capacity = device_link_table.shape[2]
    source_block = jnp.clip(device_link_table[0], 0, block_count - 1).reshape(-1)
    matrix_slot_index = jnp.clip(
        device_link_table[2], 0, remap_weight_matrices.shape[0] - 1
    ).reshape(-1)
    is_live = (device_link_table[0] >= 0).reshape(-1)

    def product(entry):
        picked_block, picked_slot, picked_live = entry
        message = jnp.dot(
            blocks[picked_block],
            remap_weight_matrices[picked_slot],
            precision=highest,
            preferred_element_type=jnp.float32,
        )
        return jnp.where(picked_live, message, jnp.zeros_like(message))

    messages = lax.map(product, (source_block, matrix_slot_index, is_live), batch_size=64)
    messages = messages.reshape(peer_count, capacity, fields, block_width)
    targets = device_link_table[1].astype(jnp.float32)
    arrived, arrived_targets = (
        lax.all_to_all(messages, ("comp", "dom"), split_axis=0, concat_axis=0, tiled=True),
        lax.all_to_all(targets, ("comp", "dom"), split_axis=0, concat_axis=0, tiled=True),
    )
    entries = peer_count * capacity
    arrived = arrived.reshape(entries, fields, block_width)
    target_index = arrived_targets.reshape(entries).astype(jnp.int32)
    one_hot = (target_index[None, :] == jnp.arange(block_count, dtype=jnp.int32)[:, None]).astype(
        jnp.float32
    )
    gathered = jnp.einsum("be,efc->bfc", one_hot, arrived, precision=highest)
    forcing_next = gathered.transpose(1, 0, 2).reshape(fields, columns)
    forcing_term = (
        jnp.dot(inject[0], forcing, precision=highest, preferred_element_type=jnp.float32)
        * wet_cells
        * DT
    )
    field = state
    for substep in range(SUBS):
        padded = with_halo(field, (("dom", 1),), 1)
        spread_term = padded[:, :-2] + padded[:, 2:] - 2.0 * field
        tendency = jnp.dot(
            vertical[0], field, precision=highest, preferred_element_type=jnp.float32
        )
        updated = field + diffuse * spread_term + DT * tendency + forcing_term
        field = jnp.where(substeps > substep, updated, field)
    return (field, forcing_next)


def solution(mesh):
    return jax.shard_map(
        local,
        mesh=mesh,
        in_specs=(
            P(None, ("comp", "dom")),
            P(None, ("comp", "dom")),
            P("comp", None, None),
            P("comp", None, None),
            P("comp", None, None),
            P(("comp", "dom")),
            P(("comp", "dom")),
            P(("comp", "dom")),
            P(None, ("comp", "dom"), None, None),
            P(("comp", "dom"), None, None),
        ),
        out_specs=(P(None, ("comp", "dom")), P(None, ("comp", "dom"))),
        check_vma=False,
    )
```

profile of v0, /device:TPU:5, one launch (start us, length us, event | category | flops | bytes accessed | tf_op | source)
XLA Modules:
  0.0 91.7 jit_solution(15919184278703958611)
XLA Ops:
  0.6 0.0 copy-start
  0.6 0.0 copy-start.2
  0.7 0.0 copy-start.3
  0.7 1.0 %fusion.51 = (f32[72,1]{1,0:T(8,128)S(1)}, f32[72,1]{1,0:T(8,128)S(1)}) fusion(f32[72,16384]{1,0:T(8,128)} %param.10), kind=kLoop, calls=%fused_computation.81 | loop fusion | bytes 1152 | tf_op jit(solution)/shard_map/slice | solution.py:16
  1.6 1.9 %collective-permute-start = (f32[72,1]{1,0:T(8,128)S(1)}, f32[72,1]{1,0:T(8,128)S(1)}, u32[]{:S(2)}, u32[]{:S(2)}) collective-permute-start(f32[72,1]{1,0:T(8,128)S(1)} %get-tuple-element.29), channel_id=1, source_target_pairs={{0,1},{1,2},{2,3},{3,4},{4,5},{5,6},{6,7},{7,0},{8,9},{9,10},{10,1... | collective-permute-start | bytes 872 | tf_op jit(solution)/shard_map/ppermute | solution.py:19
  3.5 0.0 collective-permute-start.1
  3.5 0.7 convert_bitcast_fusion
  4.2 0.7 copy.22
  4.9 6.3 %all-to-all-start = ((f32[32,1,2]{2,1,0:T(1,128)}), f32[32,1,2]{2,1,0:T(1,128)S(1)}, u32[]{:S(2)}, u32[]{:S(2)}) async-start(f32[32,1,2]{2,1,0:T(1,128)} %copy.22), calls=%async_computation | async-start | bytes 32768 | tf_op jit(solution)/shard_map/all_to_all | solution.py:75
  11.2 0.7 slice_compare_fusion
  11.9 0.8 convert_element_type.27
  12.7 0.9 broadcast_compare_fusion.3
  13.6 0.1 copy.24
  13.7 0.1 min.20
  13.8 0.1 copy.25
  13.9 0.1 min.23
  14.0 0.0 copy-start.6
  14.0 0.0 copy-start.7
  14.1 4.2 %fusion.32 = f32[128,8,128]{2,1,0:T(8,128)S(1)} fusion(f32[72,16384]{1,0:T(8,128)} %param.10, f32[16384]{0:T(1024)S(1)} %convert_element_type.27, f32[1,8,72]{2,1,0:T(8,128)} %param.14), kind=kOutput, calls=%fused_computation.49 | convolution fusion | flops 113377280 | bytes 5310720 | tf_op jit(solution)/shard_map/dot_general | solution.py:47
  18.3 0.0 copy-done.2
  18.3 0.0 copy-done.3
  18.3 5.6 %fusion.15 = f32[72,16384]{1,0:T(8,128)} fusion(f32[8,16384]{1,0:T(8,128)S(1)} %copy-done.2, f32[16384]{0:T(1024)S(1)} %convert_element_type.27, f32[1,72,8]{1,2,0:T(8,128)S(1)} %copy-done.3), kind=kOutput, calls=%fused_computation.22 | convolution fusion | flops 115605504 | bytes 5310720 | tf_op jit(solution)/shard_map/dot_general | solution.py:86
  23.9 0.1 copy.23
  24.0 0.0 collective-permute-done
  24.0 0.0 collective-permute-done.1
  24.0 0.0 copy-done.6
  24.0 0.0 copy-done.7
  24.0 11.1 %fusion.5 = f32[72,16384]{1,0:T(8,128)S(1)} fusion(f32[72,16384]{1,0:T(8,128)} %param.10, f32[72,16384]{1,0:T(8,128)} %fusion.15, f32[72,1]{1,0:T(8,128)S(1)} %collective-permute-done.1, f32[72,1]{1,0:T(8,128)S(1)} %collective-permute-done, f32[16384]{0:T(1024)S(1)} %copy-done.6, pred[16384]{0:T(1024)(128)(4,1)S(1)} %get-tuple-element.33, ...), kind=kOutput, calls=%fused_computation.11 | convolution fusion | flops 1032192000 | bytes 14259008 | tf_op jit(solution)/shard_map/dot_general | solution.py:94
  35.1 0.0 copy-start.5
  35.2 0.1 fusion.50
  35.2 1.4 %collective-permute-start.2 = (f32[72,1]{1,0:T(8,128)S(1)}, f32[72,1]{1,0:T(8,128)S(1)}, u32[]{:S(2)}, u32[]{:S(2)}) collective-permute-start(f32[72,1]{1,0:T(8,128)S(1)} %get-tuple-element.20), channel_id=1, source_target_pairs={{0,1},{1,2},{2,3},{3,4},{4,5},{5,6},{6,7},{7,0},{8,9},{9,10},{10,1... | collective-permute-start | bytes 872 | tf_op jit(solution)/shard_map/ppermute | solution.py:19
  36.7 0.6 copy-done.5
  37.3 0.4 collective-permute-start.3
  37.6 0.1 ge.9
  37.7 0.7 gather_fusion
  38.4 0.0 copy-done
  38.4 2.9 %gather_fusion.1 = f32[64,128,128]{2,1,0:T(8,128)} fusion(f32[16,128,128]{2,1,0:T(8,128)S(1)} %copy-done, s32[64]{0:T(128)S(1)} %fusion.47), kind=kCustom, calls=%fused_computation.1 | custom fusion | bytes 8389376 | tf_op jit(solution)/shard_map/while/body/eval_jaxpr/vmap()/gather | solution.py:64
  41.3 0.0 collective-permute-done.2
  41.4 0.0 collective-permute-done.3
  41.4 0.0 copy-start.1
  41.4 0.0 slice-start.1
  41.4 11.5 %fusion.8 = f32[72,16384]{1,0:T(8,128)S(1)} fusion(f32[72,16384]{1,0:T(8,128)} %copy-done.5, f32[72,16384]{1,0:T(8,128)} %fusion.15, f32[72,1]{1,0:T(8,128)S(1)} %collective-permute-done.3, f32[72,1]{1,0:T(8,128)S(1)} %collective-permute-done.2, f32[16384]{0:T(1024)S(1)} %copy-done.6, pred[16384]{0:T(1024)(128)(4,1)S(1)} %get-tuple-element.34, ...), kind=kOutput, calls=%fused_computation.14 | convolution fusion | flops 1032192000 | bytes 14259008 | tf_op jit(solution)/shard_map/dot_general | solution.py:94
  52.9 0.1 fusion.49
  53.0 1.4 %collective-permute-start.4 = (f32[72,1]{1,0:T(8,128)S(1)}, f32[72,1]{1,0:T(8,128)S(1)}, u32[]{:S(2)}, u32[]{:S(2)}) collective-permute-start(f32[72,1]{1,0:T(8,128)S(1)} %get-tuple-element.18), channel_id=1, source_target_pairs={{0,1},{1,2},{2,3},{3,4},{4,5},{5,6},{6,7},{7,0},{8,9},{9,10},{10,1... | collective-permute-start | bytes 872 | tf_op jit(solution)/shard_map/ppermute | solution.py:19
  54.4 2.0 %collective-permute-start.5 = (f32[72,1]{1,0:T(8,128)S(1)}, f32[72,1]{1,0:T(8,128)S(1)}, u32[]{:S(2)}, u32[]{:S(2)}) collective-permute-start(f32[72,1]{1,0:T(8,128)S(1)} %get-tuple-element.19), channel_id=1, source_target_pairs={{1,0},{2,1},{3,2},{4,3},{5,4},{6,5},{7,6},{0,7},{9,8},{10,9},{11,1... | collective-permute-start | bytes 872 | tf_op jit(solution)/shard_map/ppermute | solution.py:21
  56.4 4.3 %convolution_select_fusion = f32[64,8,128]{2,1,0:T(8,128)} fusion(f32[64,8,128]{2,1,0:T(8,128)S(1)} %gather_fusion, f32[64,128,128]{2,1,0:T(8,128)S(1)} %copy-done.1, pred[64]{0:T(512)(128)(4,1)S(1)} %ge.9), kind=kOutput, calls=%fused_computation.50 | convolution fusion | flops 100728832 | bytes 4718656 | tf_op jit(solution)/shard_map/while/body/eval_jaxpr/vmap()/dot_general | solution.py:62
  60.7 0.0 collective-permute-done.4
  60.7 0.0 collective-permute-done.5
  60.7 6.5 %fusion.11 = f32[72,16384]{1,0:T(8,128)S(1)} fusion(f32[72,16384]{1,0:T(8,128)S(1)} %fusion.8, f32[72,16384]{1,0:T(8,128)S(1)} %bitcast.76, f32[72,1]{1,0:T(8,128)S(1)} %collective-permute-done.5, f32[72,1]{1,0:T(8,128)S(1)} %collective-permute-done.4, f32[16384]{0:T(1024)S(1)} %copy-done.6, pred[16384]{0:T(1024)(128)(4,1)S(1)} %get-tuple-element.32, ...), kind=kOutput, calls=%fused_computation.17 | convolution fusion | flops 1032192000 | bytes 14259008 | tf_op jit(solution)/shard_map/dot_general | solution.py:94
  67.3 0.1 fusion.48
  67.4 0.0 collective-permute-start.6
  67.4 2.0 %copy-done.4 = f32[72,16384]{1,0:T(8,128)} copy-done((f32[72,16384]{1,0:T(8,128)}, f32[72,16384]{1,0:T(8,128)S(1)}, u32[]{:S(2)}) %copy-start.4) | copy-done | bytes 4718616
  69.4 3.3 %collective-permute-start.7 = (f32[72,1]{1,0:T(8,128)S(1)}, f32[72,1]{1,0:T(8,128)S(1)}, u32[]{:S(2)}, u32[]{:S(2)}) collective-permute-start(f32[72,1]{1,0:T(8,128)S(1)} %get-tuple-element.17), channel_id=1, source_target_pairs={{1,0},{2,1},{3,2},{4,3},{5,4},{6,5},{7,6},{0,7},{9,8},{10,9},{11,1... | collective-permute-start | bytes 872 | tf_op jit(solution)/shard_map/ppermute | solution.py:21
  72.7 0.0 all-to-all-done
  72.7 4.2 %all-to-all-start.1 = ((f32[32,2,8,128]{3,2,1,0:T(8,128)}), f32[32,2,8,128]{3,2,1,0:T(8,128)S(1)}, u32[]{:S(2)}, u32[]{:S(2)}) async-start(f32[32,2,8,128]{3,2,1,0:T(8,128)} %bitcast.12), calls=%async_computation.1 | async-start | bytes 524288 | tf_op jit(solution)/shard_map/all_to_all | solution.py:74
  76.9 0.1 convert_reduce_fusion
  77.0 0.1 convert_element_type.31
  77.1 0.0 collective-permute-done.6
  77.1 0.0 collective-permute-done.7
  77.1 12.8 %fusion.14 = f32[72,16384]{1,0:T(8,128)} fusion(f32[72,16384]{1,0:T(8,128)} %copy-done.4, f32[72,16384]{1,0:T(8,128)} %fusion.15, f32[72,1]{1,0:T(8,128)S(1)} %collective-permute-done.7, f32[72,1]{1,0:T(8,128)S(1)} %collective-permute-done.6, f32[16384]{0:T(1024)S(1)} %copy-done.6, pred[16384]{0:T(1024)(128)(4,1)S(1)} %get-tuple-element.31, ...), kind=kOutput, calls=%fused_computation.20 | convolution fusion | flops 1032192000 | bytes 14259008 | tf_op jit(solution)/shard_map/dot_general | solution.py:94
  89.9 0.0 all-to-all-done.1
  89.9 0.1 copy.26
  90.1 0.5 convolution_bitcast_fusion
  90.6 1.1 %copy.29 = f32[1,8,128,128]{3,1,2,0:T(8,128)} copy(f32[1,8,128,128]{3,2,1,0:T(8,128)S(1)} %convolution_bitcast_fusion) | data formatting | bytes 1048576
  (8 shorter events, 0.0 us)
Async XLA Ops:
  0.6 37.8 %copy-start = (f32[16,128,128]{2,1,0:T(8,128)S(1)}, f32[16,128,128]{2,1,0:T(8,128)}, u32[]{:S(2)}) copy-start(f32[16,128,128]{2,1,0:T(8,128)} %param.19) | copy-start | bytes 3145732
  0.6 17.6 %copy-start.2 = (f32[8,16384]{1,0:T(8,128)S(1)}, f32[8,16384]{1,0:T(8,128)}, u32[]{:S(2)}) copy-start(f32[8,16384]{1,0:T(8,128)} %param.11) | copy-start | bytes 1572868
  0.7 17.6 %copy-start.3 = (f32[1,72,8]{1,2,0:T(8,128)S(1)}, f32[1,72,8]{1,2,0:T(8,128)}, u32[]{:S(2)}) copy-start(f32[1,72,8]{1,2,0:T(8,128)} %param.13) | copy-start | bytes 6916
  1.6 22.3 %collective-permute-start = (f32[72,1]{1,0:T(8,128)S(1)}, f32[72,1]{1,0:T(8,128)S(1)}, u32[]{:S(2)}, u32[]{:S(2)}) collective-permute-start(f32[72,1]{1,0:T(8,128)S(1)} %get-tuple-element.29), channel_id=1, source_target_pairs={{0,1},{1,2},{2,3},{3,4},{4,5},{5,6},{6,7},{7,0},{8,9},{9,10},{10,1... | collective-permute-start | bytes 872 | tf_op jit(solution)/shard_map/ppermute | solution.py:19
  3.5 20.5 %collective-permute-start.1 = (f32[72,1]{1,0:T(8,128)S(1)}, f32[72,1]{1,0:T(8,128)S(1)}, u32[]{:S(2)}, u32[]{:S(2)}) collective-permute-start(f32[72,1]{1,0:T(8,128)S(1)} %get-tuple-element.30), channel_id=1, source_target_pairs={{1,0},{2,1},{3,2},{4,3},{5,4},{6,5},{7,6},{0,7},{9,8},{10,9},{11,1... | collective-permute-start | bytes 872 | tf_op jit(solution)/shard_map/ppermute | solution.py:21
  4.9 67.8 %all-to-all-start = ((f32[32,1,2]{2,1,0:T(1,128)}), f32[32,1,2]{2,1,0:T(1,128)S(1)}, u32[]{:S(2)}, u32[]{:S(2)}) async-start(f32[32,1,2]{2,1,0:T(1,128)} %copy.22), calls=%async_computation | async-start | bytes 32768 | tf_op jit(solution)/shard_map/all_to_all | solution.py:75
  14.0 10.0 %copy-start.6 = (f32[16384]{0:T(1024)S(1)}, f32[16384]{0:T(1024)}, u32[]{:S(2)}) copy-start(f32[16384]{0:T(1024)} %param.15) | copy-start | bytes 196612
  14.0 9.9 %copy-start.7 = (f32[1,72,72]{2,1,0:T(8,128)S(1)}, f32[1,72,72]{2,1,0:T(8,128)}, u32[]{:S(2)}) copy-start(f32[1,72,72]{2,1,0:T(8,128)} %param.12) | copy-start | bytes 62212
  35.1 2.1 %copy-start.5 = (f32[72,16384]{1,0:T(8,128)}, f32[72,16384]{1,0:T(8,128)S(1)}, u32[]{:S(2)}) copy-start(f32[72,16384]{1,0:T(8,128)S(1)} %fusion.5) | copy-start | bytes 14155780
  35.2 6.1 %collective-permute-start.2 = (f32[72,1]{1,0:T(8,128)S(1)}, f32[72,1]{1,0:T(8,128)S(1)}, u32[]{:S(2)}, u32[]{:S(2)}) collective-permute-start(f32[72,1]{1,0:T(8,128)S(1)} %get-tuple-element.20), channel_id=1, source_target_pairs={{0,1},{1,2},{2,3},{3,4},{4,5},{5,6},{6,7},{7,0},{8,9},{9,10},{10,1... | collective-permute-start | bytes 872 | tf_op jit(solution)/shard_map/ppermute | solution.py:19
  37.3 4.1 %collective-permute-start.3 = (f32[72,1]{1,0:T(8,128)S(1)}, f32[72,1]{1,0:T(8,128)S(1)}, u32[]{:S(2)}, u32[]{:S(2)}) collective-permute-start(f32[72,1]{1,0:T(8,128)S(1)} %get-tuple-element.28), channel_id=1, source_target_pairs={{1,0},{2,1},{3,2},{4,3},{5,4},{6,5},{7,6},{0,7},{9,8},{10,9},{11,1... | collective-permute-start | bytes 872 | tf_op jit(solution)/shard_map/ppermute | solution.py:21
  41.4 19.4 %slice-start = ((s8[4718592]{0:T(1024)(128)(4,1)}), s8[4194304]{0:T(1024)(128)(4,1)S(1)}, s32[]{:S(2)}) async-start(s8[4718592]{0:T(1024)(128)(4,1)} %bitcast.75), calls=%async_computation.2 | async-start | bytes 8388608
  41.4 15.0 %copy-start.1 = (f32[64,128,128]{2,1,0:T(8,128)S(1)}, f32[64,128,128]{2,1,0:T(8,128)}, u32[]{:S(2)}) copy-start(f32[64,128,128]{2,1,0:T(8,128)} %gather_fusion.1) | copy-start | bytes 12582916
  41.4 19.4 %slice-start.1 = ((s8[4718592]{0:T(1024)(128)(4,1)}), s8[524288]{0:T(1024)(128)(4,1)S(1)}, s32[]{:S(2)}) async-start(s8[4718592]{0:T(1024)(128)(4,1)} %bitcast.75), calls=%async_computation.3 | async-start | bytes 1048576
  53.0 7.7 %collective-permute-start.4 = (f32[72,1]{1,0:T(8,128)S(1)}, f32[72,1]{1,0:T(8,128)S(1)}, u32[]{:S(2)}, u32[]{:S(2)}) collective-permute-start(f32[72,1]{1,0:T(8,128)S(1)} %get-tuple-element.18), channel_id=1, source_target_pairs={{0,1},{1,2},{2,3},{3,4},{4,5},{5,6},{6,7},{7,0},{8,9},{9,10},{10,1... | collective-permute-start | bytes 872 | tf_op jit(solution)/shard_map/ppermute | solution.py:19
  54.4 6.3 %collective-permute-start.5 = (f32[72,1]{1,0:T(8,128)S(1)}, f32[72,1]{1,0:T(8,128)S(1)}, u32[]{:S(2)}, u32[]{:S(2)}) collective-permute-start(f32[72,1]{1,0:T(8,128)S(1)} %get-tuple-element.19), channel_id=1, source_target_pairs={{1,0},{2,1},{3,2},{4,3},{5,4},{6,5},{7,6},{0,7},{9,8},{10,9},{11,1... | collective-permute-start | bytes 872 | tf_op jit(solution)/shard_map/ppermute | solution.py:21
  67.3 2.1 %copy-start.4 = (f32[72,16384]{1,0:T(8,128)}, f32[72,16384]{1,0:T(8,128)S(1)}, u32[]{:S(2)}) copy-start(f32[72,16384]{1,0:T(8,128)S(1)} %fusion.11) | copy-start | bytes 14155780
  67.4 9.7 %collective-permute-start.6 = (f32[72,1]{1,0:T(8,128)S(1)}, f32[72,1]{1,0:T(8,128)S(1)}, u32[]{:S(2)}, u32[]{:S(2)}) collective-permute-start(f32[72,1]{1,0:T(8,128)S(1)} %get-tuple-element.16), channel_id=1, source_target_pairs={{0,1},{1,2},{2,3},{3,4},{4,5},{5,6},{6,7},{7,0},{8,9},{9,10},{10,1... | collective-permute-start | bytes 872 | tf_op jit(solution)/shard_map/ppermute | solution.py:19
  69.4 7.7 %collective-permute-start.7 = (f32[72,1]{1,0:T(8,128)S(1)}, f32[72,1]{1,0:T(8,128)S(1)}, u32[]{:S(2)}, u32[]{:S(2)}) collective-permute-start(f32[72,1]{1,0:T(8,128)S(1)} %get-tuple-element.17), channel_id=1, source_target_pairs={{1,0},{2,1},{3,2},{4,3},{5,4},{6,5},{7,6},{0,7},{9,8},{10,9},{11,1... | collective-permute-start | bytes 872 | tf_op jit(solution)/shard_map/ppermute | solution.py:21
  72.7 17.2 %all-to-all-start.1 = ((f32[32,2,8,128]{3,2,1,0:T(8,128)}), f32[32,2,8,128]{3,2,1,0:T(8,128)S(1)}, u32[]{:S(2)}, u32[]{:S(2)}) async-start(f32[32,2,8,128]{3,2,1,0:T(8,128)} %bitcast.12), calls=%async_computation.1 | async-start | bytes 524288 | tf_op jit(solution)/shard_map/all_to_all | solution.py:74
where the time goes:
time: 93.1 us; the launch traced here: 91.7 us
  matrix products  56.6 us (61%)
  starting transfers between devices  20.8 us (22%)
  local copies, waits for them, and re-layouts  10.1 us (11%)
  other arithmetic  3.19 us (3%)
    dot_general x4, matrix products, local(): jnp.dot(vertical[0], field, precision=highest, preferred_element_type=jnp...  42 us
    all_to_all x1, starting transfers between devices, local(): lax.all_to_all(targets, ('comp', 'dom'), split_axis=0, concat_axis=0, til...  6.3 us
    ppermute x4, starting transfers between devices, with_halo(): lax.ppermute(head, axis, [((i + 1) % count, i) for i in range(count)])  5.63 us
    dot_general x1, matrix products, local(): jnp.dot(inject[0], forcing, precision=highest, preferred_element_type=jnp...  5.57 us
    ppermute x4, starting transfers between devices, with_halo(): lax.ppermute(tail, axis, [(i, (i + 1) % count) for i in range(count)])  4.69 us
    dot_general x1, matrix products, product(): jnp.dot(blocks[picked_block], remap_weight_matrices[picked_slot], precisi...  4.33 us
    dot_general x1, matrix products, local(): jnp.dot(extract[0], state, precision=highest, preferred_element_type=jnp....  4.21 us
    all_to_all x1, starting transfers between devices, local(): lax.all_to_all(messages, ('comp', 'dom'), split_axis=0, concat_axis=0, ti...  4.19 us
  transfers between devices with their start and end apart: 10, of which 0 were waited for; matrix products, arithmetic and copies ran while one was open for 70% of the time, Pallas kernels for 0%

commit v1 on v0

v1 whole, which is shorter than its diff:
```python
import functools

import jax
import jax.numpy as jnp
from jax import lax
from jax.experimental import pallas as pl
from jax.experimental.pallas import tpu as pltpu
from jax.sharding import PartitionSpec as P

SUBS = 4
DT = 0.25
LANES = 128
WIDE = 256
LEAD = 512
GROUP = 8
CHUNK = 8
PAD_ROWS = 80
MESH = pl.DeviceIdType.MESH
F32 = jnp.float32
BF16 = jnp.bfloat16


def high_low(x):
    high = x.astype(BF16)
    return high, (x - high.astype(F32)).astype(BF16)


def stack_left(matrix, scratch, width):
    high = matrix.astype(BF16).astype(F32)
    low = matrix - high
    scratch[...] = jnp.zeros_like(scratch)
    size = matrix.shape[1]
    scratch[:, 0:size] = high
    scratch[:, width : width + size] = high
    scratch[:, 2 * width : 2 * width + size] = low


def exchange_kernel(
    comps,
    doms,
    links,
    state,
    forcing,
    extract,
    diffuse,
    substeps,
    landmask,
    weights,
    arrived,
    targets,
    halo,
    state_v,
    rows_v,
    edge_f,
    weights_v,
    split_w,
    left_f,
    msg,
    tgt,
    edge,
    state_sem,
    load_sem,
    edge_sem,
    msg_send,
    msg_recv,
    tgt_send,
    tgt_recv,
    halo_send,
    halo_recv,
):
    levels, columns = state.shape
    comp = lax.axis_index("comp")
    dom = lax.axis_index("dom")
    me = comp * doms + dom
    air = (comps - 1) * doms
    is_air = comp < comps - 1
    count = jnp.where(is_air, doms, air)
    first = jnp.where(is_air, air, 0)
    right = lax.rem(dom + 1, doms)
    left = lax.rem(dom + doms - 1, doms)

    span = CHUNK * WIDE
    pieces = columns // span

    def load(c):
        here = pl.ds(pl.multiple_of(c * span, span), span)
        return pltpu.make_async_copy(state.at[:, here], state_v.at[:, here], state_sem.at[c])

    load(pieces - 1).start()
    for c in range(pieces - 1):
        load(c).start()
    load_weights = pltpu.make_async_copy(weights, weights_v, load_sem)
    load_weights.start()
    edges = [
        pltpu.make_async_copy(forcing.at[:, pl.ds(at, LANES)], edge_f.at[k], edge_sem.at[k])
        for k, at in enumerate((columns - LANES, 0))
    ]
    for copy in edges:
        copy.start()

    barrier = pltpu.get_barrier_semaphore()
    for side in (left, right):
        pl.semaphore_signal(barrier, inc=1, device_id=(comp, side), device_id_type=MESH)

    def greet(p, carry):
        peer = first + p
        pl.semaphore_signal(
            barrier, inc=1, device_id=(peer // doms, peer % doms), device_id_type=MESH
        )
        return carry

    lax.fori_loop(0, count, greet, 0)

    stack_left(extract[0], left_f, PAD_ROWS)
    left_b = left_f[...].astype(BF16)[:, : 3 * PAD_ROWS]

    for copy in edges:
        copy.wait()
    load(pieces - 1).wait()
    load(0).wait()
    for k, at in enumerate((columns - LANES, 0)):
        here = slice(at, at + LANES)
        edge[k, 0:levels] = state_v[:, here]
        edge[k, levels : levels + 8] = edge_f[k] * landmask[:, here].astype(F32)
        edge[k, levels + 8 : levels + 16] = jnp.broadcast_to(diffuse[:, here], (8, LANES))
        edge[k, levels + 16 : levels + 24] = jnp.broadcast_to(
            substeps[:, here].astype(F32), (8, LANES)
        )
    pl.semaphore_wait(barrier, count + 2)
    sides = [
        pltpu.make_async_remote_copy(
            src_ref=edge.at[k],
            dst_ref=halo.at[k],
            send_sem=halo_send.at[k],
            recv_sem=halo_recv.at[k],
            device_id=(comp, side),
            device_id_type=MESH,
        )
        for k, side in enumerate((right, left))
    ]
    for copy in sides:
        copy.start()

    for c in range(pieces):
        if 0 < c < pieces - 1:
            load(c).wait()

        def extract_rows(t, carry):
            for u in range(4):
                tile = c * CHUNK + t * 4 + u
                here = pl.ds(pl.multiple_of(tile * WIDE, WIDE), WIDE)
                x = jnp.concatenate(
                    [state_v[:, here], jnp.zeros((PAD_ROWS - levels, WIDE), F32)], axis=0
                )
                high, low = high_low(x)
                r = jnp.dot(
                    left_b, jnp.concatenate([high, low, high], axis=0), preferred_element_type=F32
                )
                r = r * landmask[:, here].astype(F32)
                rows_v[2 * tile] = r[:, 0:LANES]
                rows_v[2 * tile + 1] = r[:, LANES:WIDE]
            return carry

        lax.fori_loop(0, CHUNK // 4, extract_rows, 0)
    load_weights.wait()

    def split(s, carry):
        high, low = high_low(weights_v[s])
        split_w[s, 0:LANES] = high
        split_w[s, LANES:WIDE] = low
        return carry

    lax.fori_loop(0, weights_v.shape[0], split, 0)

    def send(p):
        peer = first + p
        spot = (peer // doms, peer % doms)
        return (
            pltpu.make_async_remote_copy(
                src_ref=msg.at[p],
                dst_ref=arrived.at[me],
                send_sem=msg_send.at[p],
                recv_sem=msg_recv.at[me],
                device_id=spot,
                device_id_type=MESH,
            ),
            pltpu.make_async_remote_copy(
                src_ref=tgt.at[p],
                dst_ref=targets.at[me],
                send_sem=tgt_send.at[p],
                recv_sem=tgt_recv.at[me],
                device_id=spot,
                device_id_type=MESH,
            ),
        )

    lane = lax.broadcasted_iota(jnp.int32, (1, LANES), 1)

    def group(step, carry):
        for q in range(GROUP):
            p = step * GROUP + q
            peer = first + p
            for k in range(2):
                r = rows_v[jnp.maximum(links[0, 0, peer, k], 0)]
                high = r.astype(BF16).astype(F32)
                low = r - high
                top = jnp.concatenate([high, high], axis=1)
                bottom = jnp.concatenate([low, jnp.zeros_like(low)], axis=1)
                lhs = jnp.concatenate([top, bottom], axis=0).astype(BF16)
                slot = jnp.maximum(links[2, 0, peer, k], 0)
                out = jnp.dot(lhs, split_w[slot], preferred_element_type=F32)
                msg[p, k * 8 : (k + 1) * 8] = out[0:8] + out[8:16]
            t0 = jnp.where(lane == 0, links[1, 0, peer, 0], -1)
            tgt[p] = jnp.where(lane == 1, links[1, 0, peer, 1], t0)
            for copy in send(p):
                copy.start()
        return carry

    lax.fori_loop(0, count // GROUP, group, 0)

    def finish(p, carry):
        for copy in send(p):
            copy.wait_send()
        g = first + p
        pltpu.make_async_copy(arrived.at[g], arrived.at[g], msg_recv.at[g]).wait()
        pltpu.make_async_copy(targets.at[g], targets.at[g], tgt_recv.at[g]).wait()
        return carry

    lax.fori_loop(0, count, finish, 0)
    for copy in sides:
        copy.wait()


def exchange(comps, doms, links, state, forcing, extract, diffuse, substeps, landmask, weights):
    levels, columns = state.shape
    fields = forcing.shape[0]
    slots = weights.shape[0]
    devices = comps * doms
    peers = max(doms, devices - doms)
    anywhere = pl.BlockSpec(memory_space=pl.ANY)
    vmem = pl.BlockSpec(memory_space=pltpu.VMEM)
    smem = pl.BlockSpec(memory_space=pltpu.SMEM)
    edge_rows = levels + 24
    return pl.pallas_call(
        functools.partial(exchange_kernel, comps, doms),
        out_shape=(
            jax.ShapeDtypeStruct((devices, 2 * fields, LANES), F32),
            jax.ShapeDtypeStruct((devices, 1, LANES), jnp.int32),
            jax.ShapeDtypeStruct((2, edge_rows, LANES), F32),
        ),
        in_specs=[smem, anywhere, anywhere, vmem, vmem, vmem, vmem, anywhere],
        out_specs=(anywhere, anywhere, anywhere),
        scratch_shapes=[
            pltpu.VMEM((levels, columns), F32),
            pltpu.VMEM((columns // LANES, fields, LANES), F32),
            pltpu.VMEM((2, fields, LANES), F32),
            pltpu.VMEM(weights.shape, F32),
            pltpu.VMEM((slots, WIDE, LANES), BF16),
            pltpu.VMEM((fields, WIDE), F32),
            pltpu.VMEM((peers, 2 * fields, LANES), F32),
            pltpu.VMEM((peers, 1, LANES), jnp.int32),
            pltpu.VMEM((2, edge_rows, LANES), F32),
            pltpu.SemaphoreType.DMA((columns // (CHUNK * WIDE),)),
            pltpu.SemaphoreType.DMA,
            pltpu.SemaphoreType.DMA((2,)),
            pltpu.SemaphoreType.DMA((peers,)),
            pltpu.SemaphoreType.DMA((devices,)),
            pltpu.SemaphoreType.DMA((peers,)),
            pltpu.SemaphoreType.DMA((devices,)),
            pltpu.SemaphoreType.DMA((2,)),
            pltpu.SemaphoreType.DMA((2,)),
        ],
        compiler_params=pltpu.CompilerParams(
            collective_id=0, has_side_effects=True, vmem_limit_bytes=24 << 20
        ),
        name="exchange",
    )(links, state, forcing, extract, diffuse, substeps, landmask, weights)


def advance_kernel(
    comps,
    doms,
    targets,
    state,
    forcing,
    vertical,
    inject,
    diffuse,
    substeps,
    landmask,
    arrived,
    halo,
    state_next,
    forcing_next,
    fields_v,
    out_v,
    force_v,
    next_v,
    mix_v,
    sub_v,
    left_f,
    load_sem,
    store_sem,
    next_sem,
):
    levels, columns = state.shape
    blocks = columns // WIDE
    start = LEAD // WIDE
    pieces = blocks // CHUNK
    span = CHUNK * WIDE

    def load(c):
        return pltpu.make_async_copy(
            state.at[:, pl.ds(pl.multiple_of(c * span, span), span)],
            fields_v.at[0, :, pl.ds(pl.multiple_of(c * span + LEAD, LANES), span)],
            load_sem.at[c],
        )

    def store(c):
        here = pl.ds(pl.multiple_of(c * span, span), span)
        return pltpu.make_async_copy(out_v.at[:, here], state_next.at[:, here], store_sem.at[c])

    for c in range(pieces):
        load(c).start()

    left_f[...] = jnp.zeros_like(left_f)
    high_v = (vertical[0] * DT).astype(BF16).astype(F32)
    low_v = vertical[0] * DT - high_v
    high_i = (inject[0] * DT).astype(BF16).astype(F32)
    low_i = inject[0] * DT - high_i
    for k, (v, f) in enumerate(((high_v, high_i), (high_v, high_i), (low_v, low_i))):
        at = k * PAD_ROWS
        left_f[:, at : at + levels] = v
        left_f[:, at + levels : at + PAD_ROWS] = f
    left_b = left_f[...].astype(BF16)[:, : 3 * PAD_ROWS]

    tail = LEAD + columns
    here = slice(LEAD, tail)
    force_v[:, here] = forcing[...] * landmask[...].astype(F32)
    mix_v[:, here] = diffuse[...]
    sub_v[:, here] = substeps[...]
    for k, at in enumerate((LEAD - LANES, tail)):
        there = slice(at, at + LANES)
        fields_v[0, :, there] = halo[k, 0:levels]
        force_v[:, there] = halo[k, levels : levels + 8]
        mix_v[:, there] = halo[k, levels + 8 : levels + 9]
        sub_v[:, there] = halo[k, levels + 16 : levels + 17].astype(jnp.int32)

    next_v[...] = jnp.zeros_like(next_v)
    air = (comps - 1) * doms
    is_air = lax.axis_index("comp") < comps - 1
    count = jnp.where(is_air, doms, air)
    first = jnp.where(is_air, air, 0)

    def scatter(p, carry):
        for k in range(2):
            t = targets[first + p, 0, k]
            there = pl.ds(pl.multiple_of(jnp.maximum(t, 0) * LANES, LANES), LANES)
            part = arrived[first + p, k * 8 : (k + 1) * 8]
            next_v[:, there] += jnp.where(t >= 0, part, jnp.zeros_like(part))
        return carry

    lax.fori_loop(0, count, scatter, 0)
    store_next = pltpu.make_async_copy(next_v, forcing_next, next_sem)
    store_next.start()

    lane = lax.broadcasted_iota(jnp.int32, (levels, LANES), 1)
    at_first = lane == 0
    at_last = lane == LANES - 1

    def update(j, b):
        base = b * WIDE
        if not isinstance(b, int):
            base = pl.multiple_of(base, WIDE)

        def piece(k):
            return fields_v[j, :, pl.ds(base + (k - 1) * LANES, LANES)]

        near = [piece(k) for k in range(4)]
        back = [pltpu.roll(near[k], 1, axis=1) for k in range(3)]
        ahead = [pltpu.roll(near[k], LANES - 1, axis=1) for k in range(1, 4)]
        here = pl.ds(base, WIDE)
        x = jnp.concatenate(near[1:3], axis=1)
        both = jnp.concatenate(
            [
                jnp.where(at_first, back[k], back[k + 1]) + jnp.where(at_last, ahead[k + 1], ahead[k])
                for k in range(2)
            ],
            axis=1,
        )
        high, low = high_low(jnp.concatenate([x, force_v[:, here]], axis=0))
        change = jnp.dot(
            left_b, jnp.concatenate([high, low, high], axis=0), preferred_element_type=F32
        )
        d = mix_v[:, here]
        new = (1.0 - 2.0 * d) * x + (d * both + change)
        if j > 0:
            new = jnp.where(sub_v[:, here] > j, new, x)
        if j < SUBS - 1:
            fields_v[j + 1, :, here] = new
        else:
            there = base - LEAD
            if not isinstance(b, int):
                there = pl.multiple_of(there, WIDE)
            out_v[:, pl.ds(there, WIDE)] = new

    low_b, high_b = start - 1, start + blocks

    def valid(i, j):
        b = i - 2 * j
        if j == SUBS - 1:
            return start <= b < start + blocks
        return low_b <= b <= high_b

    body_from = low_b + 2 * (SUBS - 1) + 1
    body_to = high_b + 1
    waited = 0
    last = start + blocks - 1 + 2 * (SUBS - 1)
    for i in range(low_b, body_from):
        while waited < pieces and waited * CHUNK + start <= i + 1:
            load(waited).wait()
            waited += 1
        for j in range(SUBS):
            if valid(i, j):
                update(j, i - 2 * j)

    def body(i, carry):
        coming = i + 1 - start

        @pl.when((coming % CHUNK == 0) & (coming // CHUNK >= waited) & (coming // CHUNK < pieces))
        def _():
            load(coming // CHUNK).wait()

        for j in range(SUBS):
            update(j, i - 2 * j)
        ended = i - 2 * (SUBS - 1) - start + 1

        @pl.when(ended % CHUNK == 0)
        def _():
            store(ended // CHUNK - 1).start()

        return carry

    lax.fori_loop(body_from, body_to, body, 0)
    for i in range(body_to, last + 1):
        for j in range(SUBS):
            if valid(i, j):
                update(j, i - 2 * j)
    for c in range((body_to - 1 - 2 * (SUBS - 1) - start + 1) // CHUNK, pieces):
        store(c).start()
    for c in range(pieces):
        store(c).wait()
    store_next.wait()


def advance(comps, doms, targets, state, forcing, vertical, inject, diffuse, substeps, landmask, arrived, halo):
    levels, columns = state.shape
    fields = forcing.shape[0]
    width = columns + 2 * LEAD
    pieces = columns // (CHUNK * WIDE)
    anywhere = pl.BlockSpec(memory_space=pl.ANY)
    vmem = pl.BlockSpec(memory_space=pltpu.VMEM)
    smem = pl.BlockSpec(memory_space=pltpu.SMEM)
    return pl.pallas_call(
        functools.partial(advance_kernel, comps, doms),
        out_shape=(
            jax.ShapeDtypeStruct(state.shape, F32),
            jax.ShapeDtypeStruct(forcing.shape, F32),
        ),
        in_specs=[smem, anywhere] + [vmem] * 8,
        out_specs=(anywhere, anywhere),
        scratch_shapes=[
            pltpu.VMEM((SUBS, levels, width), F32),
            pltpu.VMEM((levels, columns), F32),
            pltpu.VMEM((fields, width), F32),
            pltpu.VMEM((fields, columns), F32),
            pltpu.VMEM((1, width), F32),
            pltpu.VMEM((1, width), jnp.int32),
            pltpu.VMEM((levels, WIDE), F32),
            pltpu.SemaphoreType.DMA((pieces,)),
            pltpu.SemaphoreType.DMA((pieces,)),
            pltpu.SemaphoreType.DMA,
        ],
        compiler_params=pltpu.CompilerParams(vmem_limit_bytes=48 << 20),
        name="advance",
    )(targets, state, forcing, vertical, inject, diffuse, substeps, landmask, arrived, halo)


def solution(mesh):
    comps, doms = mesh.shape["comp"], mesh.shape["dom"]

    def local(state, forcing, vertical, inject, extract, diffuse, substeps, landmask, links, weights):
        rows = [a.reshape(1, -1) for a in (diffuse, substeps, landmask)]
        arrived, targets, halo = exchange(
            comps, doms, links, state, forcing, extract, *rows, weights
        )
        return advance(
            comps, doms, targets, state, forcing, vertical, inject, *rows, arrived, halo
        )

    return jax.shard_map(
        local,
        mesh=mesh,
        in_specs=(
            P(None, ("comp", "dom")),
            P(None, ("comp", "dom")),
            P("comp", None, None),
            P("comp", None, None),
            P("comp", None, None),
            P(("comp", "dom")),
            P(("comp", "dom")),
            P(("comp", "dom")),
            P(None, ("comp", "dom"), None, None),
            P(("comp", "dom"), None, None),
        ),
        out_specs=(P(None, ("comp", "dom")), P(None, ("comp", "dom"))),
        check_vma=False,
    )
```

time: 93.1 us -> 72.5 us (0.78); the launches traced: 91.7 us -> 72 us
  Pallas kernels: 0 us -> 61.9 us
  matrix products: 56.6 us -> 0 us
  starting transfers between devices: 20.8 us -> 0 us
  other arithmetic: 3.19 us -> 0 us
    pallas_call x0 -> x2, Pallas kernels: none -> 61.9 us  [the longest x1 45.2 us: advance(): pl.pallas_call(functools.partial(advance_kernel, comps, doms), out_shape=...]
    dot_general x8 -> x0, matrix products: 56.6 us -> none  [the longest x4 42 us: local(): jnp.dot(vertical[0], field, precision=highest, preferred_element_type=jnp...]
    all_to_all x2 -> x0, starting transfers between devices: 10.5 us -> none  [the longest x1 6.3 us: local(): lax.all_to_all(targets, ('comp', 'dom'), split_axis=0, concat_axis=0, til...]
    ppermute x8 -> x0, starting transfers between devices: 10.3 us -> none  [the longest x4 5.63 us: with_halo(): lax.ppermute(head, axis, [((i + 1) % count, i) for i in range(count)])]
    unnamed x21 -> x28, local copies, waits for them, and re-layouts: 3.81 us -> 9.41 us
    gather x2 -> x0, local copies, waits for them, and re-layouts: 3.58 us -> none  [the longest x1 2.91 us: product(): remap_weight_matrices[picked_slot]]
    convert_element_type x3 -> x0, other arithmetic: 1.61 us -> none  [the longest x1 0.84 us: local(): wet_cells = landmask.astype(jnp.float32)]
    slice x4 -> x0, local copies, waits for them, and re-layouts: 1.21 us -> none  [with_halo(): lax.slice_in_dim(cells, cells.shape[dim] - width, cells.shape[dim], axis=...]
  transfers between devices with their start and end apart: 10 -> 0, of which waited for: 0 -> 0; matrix products, arithmetic and copies ran while one was open for 70% -> 0% of each run, Pallas kernels for 0% -> 0%
where the time goes in v1:
time: 72.5 us; the launch traced here: 72 us
  Pallas kernels  61.9 us (85%)
  local copies, waits for them, and re-layouts  9.41 us (13%)
    pallas_call x1, Pallas kernels, advance(): pl.pallas_call(functools.partial(advance_kernel, comps, doms), out_shape=...  45.2 us
    pallas_call x1, Pallas kernels, exchange(): pl.pallas_call(functools.partial(exchange_kernel, comps, doms), out_shape...  16.7 us
    unnamed x28, local copies, waits for them, and re-layouts  9.41 us

profile of v1, /device:TPU:5, one launch (start us, length us, event | category | flops | bytes accessed | tf_op | source)
XLA Modules:
  0.0 72.0 jit_solution(13384012235219853729)
XLA Ops:
  0.6 0.0 copy-start.6
  0.6 0.8 %copy.13.inject = f32[1,72,8]{2,1,0:T(8,128)S(1)} copy(f32[1,72,8]{1,2,0:T(8,128)} %param.13) | data formatting | bytes 4608 | tf_op args[3]
  1.4 0.8 %copy.12.links = s32[3,1,32,2]{3,2,1,0:T(8,128)S(1)} copy(s32[3,1,32,2]{2,3,1,0:T(2,128)} %param.18) | data formatting | bytes 1536 | tf_op args[8]
  2.2 0.0 copy-start
  2.2 2.3 %copy-done = f32[72,16384]{1,0:T(8,128)S(1)} copy-done((f32[72,16384]{1,0:T(8,128)S(1)}, f32[72,16384]{1,0:T(8,128)}, u32[]{:S(2)}) %copy-start) | copy-done | bytes 4718616
  4.6 0.0 copy-start.2
  4.6 1.0 %copy-done.2 = f32[8,16384]{1,0:T(8,128)S(1)} copy-done((f32[8,16384]{1,0:T(8,128)S(1)}, f32[8,16384]{1,0:T(8,128)}, u32[]{:S(2)}) %copy-start.2) | copy-done | bytes 524312
  5.6 0.0 copy-start.4
  5.6 1.2 %copy-done.4 = f32[16,128,128]{2,1,0:T(8,128)S(1)} copy-done((f32[16,128,128]{2,1,0:T(8,128)S(1)}, f32[16,128,128]{2,1,0:T(8,128)}, u32[]{:S(2)}) %copy-start.4) | copy-done | bytes 1048600
  6.8 0.0 copy-start.5
  6.8 0.8 %copy-done.5 = f32[16384]{0:T(1024)S(1)} copy-done((f32[16384]{0:T(1024)S(1)}, f32[16384]{0:T(1024)}, u32[]{:S(2)}) %copy-start.5) | copy-done | bytes 65560
  7.7 0.0 copy-start.7
  7.7 0.8 %copy-done.7 = s32[16384]{0:T(1024)S(1)} copy-done((s32[16384]{0:T(1024)S(1)}, s32[16384]{0:T(1024)}, u32[]{:S(2)}) %copy-start.7) | copy-done | bytes 65560
  8.5 0.0 copy-start.9
  8.5 0.8 %copy-done.9 = s32[16384]{0:T(1024)S(1)} copy-done((s32[16384]{0:T(1024)S(1)}, s32[16384]{0:T(1024)}, u32[]{:S(2)}) %copy-start.9) | copy-done | bytes 65560
  9.3 0.0 copy-start.12
  9.3 0.7 copy-done.12
  10.0 0.0 copy-start.1
  10.0 0.0 copy-start.3
  10.0 0.0 copy-start.8
  10.0 0.0 copy-start.10
  10.0 0.0 copy-start.11
  10.1 16.7 %exchange.1 = (f32[32,16,128]{2,1,0:T(8,128)S(1)}, s32[32,1,128]{2,1,0:T(1,128)S(1)}, f32[2,96,128]{2,1,0:T(8,128)S(1)}) custom-call(s32[3,1,32,2]{3,2,1,0:T(8,128)S(1)} %copy.12.links, f32[72,16384]{1,0:T(8,128)S(1)} %copy-done, f32[8,16384]{1,0:T(8,128)S(1)} %copy-done.2, f32[1,8,72]{2,1,0:T(8,128)S(1)} %copy-done.12, f32[1,16384]{1,0:T(1,128)S(1)} %bitcast.3, ...), custom_call_target="tpu_custom_call" | custom-call | tf_op jit(solution)/shard_map/exchange/pallas_call | solution.py:244
  26.8 0.0 copy-done.6
  26.8 0.0 copy-done.1
  26.8 0.0 copy-done.3
  26.8 0.0 copy-done.8
  26.8 0.0 copy-done.10
  26.8 0.0 copy-done.11
  26.9 45.2 %advance.1 = (f32[72,16384]{1,0:T(8,128)}, f32[8,16384]{1,0:T(8,128)}) custom-call(s32[32,1,128]{2,1,0:T(1,128)S(1)} %get-tuple-element.5.targets, f32[72,16384]{1,0:T(8,128)S(1)} %copy-done.1, f32[8,16384]{1,0:T(8,128)S(1)} %copy-done.3, f32[1,72,72]{2,1,0:T(8,128)S(1)} %copy-done.11, f32[1,72,8]{2,1,0:T(8,128)S(1)} %copy.13.inject, ...), custom_call_target="tpu_custom_call" | custom-call | tf_op jit(solution)/shard_map/advance/pallas_call | solution.py:464
Async XLA Ops:
  0.6 26.2 %copy-start.6 = (f32[16384]{0:T(1024)S(1)}, f32[16384]{0:T(1024)}, u32[]{:S(2)}) copy-start(f32[16384]{0:T(1024)} %param.15) | copy-start | bytes 196612
  2.2 2.3 %copy-start = (f32[72,16384]{1,0:T(8,128)S(1)}, f32[72,16384]{1,0:T(8,128)}, u32[]{:S(2)}) copy-start(f32[72,16384]{1,0:T(8,128)} %state.3) | copy-start | bytes 14155780
  4.6 1.0 %copy-start.2 = (f32[8,16384]{1,0:T(8,128)S(1)}, f32[8,16384]{1,0:T(8,128)}, u32[]{:S(2)}) copy-start(f32[8,16384]{1,0:T(8,128)} %forcing.3) | copy-start | bytes 1572868
  5.6 1.2 %copy-start.4 = (f32[16,128,128]{2,1,0:T(8,128)S(1)}, f32[16,128,128]{2,1,0:T(8,128)}, u32[]{:S(2)}) copy-start(f32[16,128,128]{2,1,0:T(8,128)} %weights.1) | copy-start | bytes 3145732
  6.8 0.8 %copy-start.5 = (f32[16384]{0:T(1024)S(1)}, f32[16384]{0:T(1024)}, u32[]{:S(2)}) copy-start(f32[16384]{0:T(1024)} %param.15) | copy-start | bytes 196612
  7.7 0.8 %copy-start.7 = (s32[16384]{0:T(1024)S(1)}, s32[16384]{0:T(1024)}, u32[]{:S(2)}) copy-start(s32[16384]{0:T(1024)} %param.16) | copy-start | bytes 196612
  8.5 0.8 %copy-start.9 = (s32[16384]{0:T(1024)S(1)}, s32[16384]{0:T(1024)}, u32[]{:S(2)}) copy-start(s32[16384]{0:T(1024)} %param.17) | copy-start | bytes 196612
  9.3 0.7 copy-start.12
  10.0 16.8 %copy-start.1 = (f32[72,16384]{1,0:T(8,128)S(1)}, f32[72,16384]{1,0:T(8,128)}, u32[]{:S(2)}) copy-start(f32[72,16384]{1,0:T(8,128)} %state.3) | copy-start | bytes 14155780
  10.0 16.8 %copy-start.3 = (f32[8,16384]{1,0:T(8,128)S(1)}, f32[8,16384]{1,0:T(8,128)}, u32[]{:S(2)}) copy-start(f32[8,16384]{1,0:T(8,128)} %forcing.3) | copy-start | bytes 1572868
  10.0 16.8 %copy-start.8 = (s32[16384]{0:T(1024)S(1)}, s32[16384]{0:T(1024)}, u32[]{:S(2)}) copy-start(s32[16384]{0:T(1024)} %param.16) | copy-start | bytes 196612
  10.0 16.8 %copy-start.10 = (s32[16384]{0:T(1024)S(1)}, s32[16384]{0:T(1024)}, u32[]{:S(2)}) copy-start(s32[16384]{0:T(1024)} %param.17) | copy-start | bytes 196612
  10.0 16.8 %copy-start.11 = (f32[1,72,72]{2,1,0:T(8,128)S(1)}, f32[1,72,72]{2,1,0:T(8,128)}, u32[]{:S(2)}) copy-start(f32[1,72,72]{2,1,0:T(8,128)} %vertical.1) | copy-start | bytes 62212

commit v2 on v1

--- a/solution.py
+++ b/solution.py
@@ -11,7 +11,9 @@
 DT = 0.25
 LANES = 128
 WIDE = 256
-LEAD = 512
+STRIP = 256
+LEAD = 2 * STRIP
+STRIPS = 2048 // STRIP
 GROUP = 8
 CHUNK = 8
 PAD_ROWS = 80
@@ -51,7 +53,11 @@
     halo,
     state_v,
     rows_v,
+    extract_v,
+    wet_v,
     edge_f,
+    edge_d,
+    edge_n,
     weights_v,
     split_w,
     left_f,
@@ -92,9 +98,16 @@
     load_weights = pltpu.make_async_copy(weights, weights_v, load_sem)
     load_weights.start()
     edges = [
-        pltpu.make_async_copy(forcing.at[:, pl.ds(at, LANES)], edge_f.at[k], edge_sem.at[k])
-        for k, at in enumerate((columns - LANES, 0))
+        pltpu.make_async_copy(extract.at[0], extract_v, edge_sem.at[0]),
+        pltpu.make_async_copy(landmask, wet_v, edge_sem.at[1]),
     ]
+    for k, at in enumerate((columns - LANES, 0)):
+        for m, (src, dst) in enumerate(((forcing, edge_f), (diffuse, edge_d), (substeps, edge_n))):
+            edges.append(
+                pltpu.make_async_copy(
+                    src.at[:, pl.ds(at, LANES)], dst.at[k], edge_sem.at[2 + 3 * k + m]
+                )
+            )
     for copy in edges:
         copy.start()
 
@@ -111,20 +124,19 @@
 
     lax.fori_loop(0, count, greet, 0)
 
-    stack_left(extract[0], left_f, PAD_ROWS)
-    left_b = left_f[...].astype(BF16)[:, : 3 * PAD_ROWS]
-
     for copy in edges:
         copy.wait()
+    stack_left(extract_v[...], left_f, PAD_ROWS)
+    left_b = left_f[...].astype(BF16)[:, : 3 * PAD_ROWS]
     load(pieces - 1).wait()
     load(0).wait()
     for k, at in enumerate((columns - LANES, 0)):
         here = slice(at, at + LANES)
         edge[k, 0:levels] = state_v[:, here]
-        edge[k, levels : levels + 8] = edge_f[k] * landmask[:, here].astype(F32)
-        edge[k, levels + 8 : levels + 16] = jnp.broadcast_to(diffuse[:, here], (8, LANES))
+        edge[k, levels : levels + 8] = edge_f[k] * wet_v[:, here].astype(F32)
+        edge[k, levels + 8 : levels + 16] = jnp.broadcast_to(edge_d[k], (8, LANES))
         edge[k, levels + 16 : levels + 24] = jnp.broadcast_to(
-            substeps[:, here].astype(F32), (8, LANES)
+            edge_n[k].astype(F32), (8, LANES)
         )
     pl.semaphore_wait(barrier, count + 2)
     sides = [
@@ -145,23 +157,21 @@
         if 0 < c < pieces - 1:
             load(c).wait()
 
-        def extract_rows(t, carry):
-            for u in range(4):
-                tile = c * CHUNK + t * 4 + u
-                here = pl.ds(pl.multiple_of(tile * WIDE, WIDE), WIDE)
-                x = jnp.concatenate(
-                    [state_v[:, here], jnp.zeros((PAD_ROWS - levels, WIDE), F32)], axis=0
-                )
-                high, low = high_low(x)
-                r = jnp.dot(
-                    left_b, jnp.concatenate([high, low, high], axis=0), preferred_element_type=F32
-                )
-                r = r * landmask[:, here].astype(F32)
-                rows_v[2 * tile] = r[:, 0:LANES]
-                rows_v[2 * tile + 1] = r[:, LANES:WIDE]
-            return carry
-
-        lax.fori_loop(0, CHUNK // 4, extract_rows, 0)
+        outs = []
+        for u in range(CHUNK):
+            here = pl.ds((c * CHUNK + u) * WIDE, WIDE)
+            x = jnp.concatenate(
+                [state_v[:, here], jnp.zeros((PAD_ROWS - levels, WIDE), F32)], axis=0
+            )
+            high, low = high_low(x)
+            r = jnp.dot(
+                left_b, jnp.concatenate([high, low, high], axis=0), preferred_element_type=F32
+            )
+            outs.append(r * wet_v[:, here].astype(F32))
+        for u in range(CHUNK):
+            tile = c * CHUNK + u
+            rows_v[2 * tile] = outs[u][:, 0:LANES]
+            rows_v[2 * tile + 1] = outs[u][:, LANES:WIDE]
     load_weights.wait()
 
     def split(s, carry):
@@ -170,7 +180,7 @@
         split_w[s, LANES:WIDE] = low
         return carry
 
-    lax.fori_loop(0, weights_v.shape[0], split, 0)
+    lax.fori_loop(0, weights_v.shape[0], split, 0, unroll=4)
 
     def send(p):
         peer = first + p
@@ -197,22 +207,27 @@
     lane = lax.broadcasted_iota(jnp.int32, (1, LANES), 1)
 
     def group(step, carry):
+        outs = []
         for q in range(GROUP):
-            p = step * GROUP + q
-            peer = first + p
+            peer = first + step * GROUP + q
             for k in range(2):
-                r = rows_v[jnp.maximum(links[0, 0, peer, k], 0)]
+                r = rows_v[jnp.maximum(links[0, 0, k, peer], 0)]
                 high = r.astype(BF16).astype(F32)
                 low = r - high
                 top = jnp.concatenate([high, high], axis=1)
                 bottom = jnp.concatenate([low, jnp.zeros_like(low)], axis=1)
                 lhs = jnp.concatenate([top, bottom], axis=0).astype(BF16)
-                slot = jnp.maximum(links[2, 0, peer, k], 0)
+                slot = jnp.maximum(links[2, 0, k, peer], 0)
                 out = jnp.dot(lhs, split_w[slot], preferred_element_type=F32)
-                msg[p, k * 8 : (k + 1) * 8] = out[0:8] + out[8:16]
-            t0 = jnp.where(lane == 0, links[1, 0, peer, 0], -1)
-            tgt[p] = jnp.where(lane == 1, links[1, 0, peer, 1], t0)
-            for copy in send(p):
+                outs.append(out[0:8] + out[8:16])
+        for q in range(GROUP):
+            p = step * GROUP + q
+            peer = first + p
+            msg[p] = jnp.concatenate(outs[2 * q : 2 * q + 2], axis=0)
+            t0 = jnp.where(lane == 0, links[1, 0, 0, peer], -1)
+            tgt[p] = jnp.where(lane == 1, links[1, 0, 1, peer], t0)
+        for q in range(GROUP):
+            for copy in send(step * GROUP + q):
                 copy.start()
         return carry
 
@@ -237,8 +252,7 @@
     slots = weights.shape[0]
     devices = comps * doms
     peers = max(doms, devices - doms)
-    anywhere = pl.BlockSpec(memory_space=pl.ANY)
-    vmem = pl.BlockSpec(memory_space=pltpu.VMEM)
+    hbm = pl.BlockSpec(memory_space=pltpu.HBM)
     smem = pl.BlockSpec(memory_space=pltpu.SMEM)
     edge_rows = levels + 24
     return pl.pallas_call(
@@ -248,12 +262,16 @@
             jax.ShapeDtypeStruct((devices, 1, LANES), jnp.int32),
             jax.ShapeDtypeStruct((2, edge_rows, LANES), F32),
         ),
-        in_specs=[smem, anywhere, anywhere, vmem, vmem, vmem, vmem, anywhere],
-        out_specs=(anywhere, anywhere, anywhere),
+        in_specs=[smem] + [hbm] * 7,
+        out_specs=(hbm, hbm, hbm),
         scratch_shapes=[
             pltpu.VMEM((levels, columns), F32),
             pltpu.VMEM((columns // LANES, fields, LANES), F32),
+            pltpu.VMEM((fields, levels), F32),
+            pltpu.VMEM((1, columns), jnp.int32),
             pltpu.VMEM((2, fields, LANES), F32),
+            pltpu.VMEM((2, 1, LANES), F32),
+            pltpu.VMEM((2, 1, LANES), jnp.int32),
             pltpu.VMEM(weights.shape, F32),
             pltpu.VMEM((slots, WIDE, LANES), BF16),
             pltpu.VMEM((fields, WIDE), F32),
@@ -262,7 +280,7 @@
             pltpu.VMEM((2, edge_rows, LANES), F32),
             pltpu.SemaphoreType.DMA((columns // (CHUNK * WIDE),)),
             pltpu.SemaphoreType.DMA,
-            pltpu.SemaphoreType.DMA((2,)),
+            pltpu.SemaphoreType.DMA((8,)),
             pltpu.SemaphoreType.DMA((peers,)),
             pltpu.SemaphoreType.DMA((devices,)),
             pltpu.SemaphoreType.DMA((peers,)),
@@ -271,7 +289,7 @@
             pltpu.SemaphoreType.DMA((2,)),
         ],
         compiler_params=pltpu.CompilerParams(
-            collective_id=0, has_side_effects=True, vmem_limit_bytes=24 << 20
+            collective_id=0, has_side_effects=True, vmem_limit_bytes=60 << 20
         ),
         name="exchange",
     )(links, state, forcing, extract, diffuse, substeps, landmask, weights)
@@ -292,27 +310,37 @@
     halo,
     state_next,
     forcing_next,
-    fields_v,
+    field_0,
+    field_1,
+    field_2,
+    field_3,
     out_v,
     force_v,
     next_v,
     mix_v,
     sub_v,
+    wet_v,
+    vertical_v,
+    inject_v,
+    arrived_v,
+    halo_v,
     left_f,
     load_sem,
     store_sem,
     next_sem,
+    small_sem,
 ):
     levels, columns = state.shape
-    blocks = columns // WIDE
-    start = LEAD // WIDE
-    pieces = blocks // CHUNK
-    span = CHUNK * WIDE
+    chain = (field_0, field_1, field_2, field_3)
+    blocks = columns // STRIP
+    start = LEAD // STRIP
+    pieces = blocks // STRIPS
+    span = STRIPS * STRIP
 
     def load(c):
         return pltpu.make_async_copy(
             state.at[:, pl.ds(pl.multiple_of(c * span, span), span)],
-            fields_v.at[0, :, pl.ds(pl.multiple_of(c * span + LEAD, LANES), span)],
+            field_0.at[:, pl.ds(pl.multiple_of(c * span + LEAD, LANES), span)],
             load_sem.at[c],
         )
 
@@ -320,33 +348,53 @@
         here = pl.ds(pl.multiple_of(c * span, span), span)
         return pltpu.make_async_copy(out_v.at[:, here], state_next.at[:, here], store_sem.at[c])
 
-    for c in range(pieces):
+    tail = LEAD + columns
+    here = slice(LEAD, tail)
+    small = [
+        pltpu.make_async_copy(src, dst, small_sem.at[k])
+        for k, (src, dst) in enumerate(
+            (
+                (vertical.at[0], vertical_v),
+                (inject.at[0], inject_v),
+                (halo, halo_v),
+                (diffuse, mix_v.at[:, pl.ds(LEAD, columns)]),
+                (substeps, sub_v.at[:, pl.ds(LEAD, columns)]),
+                (landmask, wet_v),
+                (forcing, force_v.at[:, pl.ds(LEAD, columns)]),
+                (arrived, arrived_v),
+            )
+        )
+    ]
+    for copy in small[:3]:
+        copy.start()
+    load(0).start()
+    for copy in small[3:]:
+        copy.start()
+    for c in range(1, pieces):
         load(c).start()
-
+    next_v[...] = jnp.zeros_like(next_v)
     left_f[...] = jnp.zeros_like(left_f)
-    high_v = (vertical[0] * DT).astype(BF16).astype(F32)
-    low_v = vertical[0] * DT - high_v
-    high_i = (inject[0] * DT).astype(BF16).astype(F32)
-    low_i = inject[0] * DT - high_i
+    for copy in small:
+        copy.wait()
+    high_v = (vertical_v[...] * DT).astype(BF16).astype(F32)
+    low_v = vertical_v[...] * DT - high_v
+    inject_t = jnp.transpose(inject_v[...])[0:levels] * DT
+    high_i = inject_t.astype(BF16).astype(F32)
+    low_i = inject_t - high_i
     for k, (v, f) in enumerate(((high_v, high_i), (high_v, high_i), (low_v, low_i))):
         at = k * PAD_ROWS
         left_f[:, at : at + levels] = v
         left_f[:, at + levels : at + PAD_ROWS] = f
     left_b = left_f[...].astype(BF16)[:, : 3 * PAD_ROWS]
 
-    tail = LEAD + columns
-    here = slice(LEAD, tail)
-    force_v[:, here] = forcing[...] * landmask[...].astype(F32)
-    mix_v[:, here] = diffuse[...]
-    sub_v[:, here] = substeps[...]
+    force_v[:, here] = force_v[:, here] * wet_v[...].astype(F32)
     for k, at in enumerate((LEAD - LANES, tail)):
         there = slice(at, at + LANES)
-        fields_v[0, :, there] = halo[k, 0:levels]
-        force_v[:, there] = halo[k, levels : levels + 8]
-        mix_v[:, there] = halo[k, levels + 8 : levels + 9]
-        sub_v[:, there] = halo[k, levels + 16 : levels + 17].astype(jnp.int32)
-
-    next_v[...] = jnp.zeros_like(next_v)
+        field_0[:, there] = halo_v[k, 0:levels]
+        force_v[:, there] = halo_v[k, levels : levels + 8]
+        mix_v[:, there] = halo_v[k, levels + 8 : levels + 9]
+        sub_v[:, there] = halo_v[k, levels + 16 : levels + 17].astype(jnp.int32)
+
     air = (comps - 1) * doms
     is_air = lax.axis_index("comp") < comps - 1
     count = jnp.where(is_air, doms, air)
@@ -356,7 +404,7 @@
         for k in range(2):
             t = targets[first + p, 0, k]
             there = pl.ds(pl.multiple_of(jnp.maximum(t, 0) * LANES, LANES), LANES)
-            part = arrived[first + p, k * 8 : (k + 1) * 8]
+            part = arrived_v[first + p, k * 8 : (k + 1) * 8]
             next_v[:, there] += jnp.where(t >= 0, part, jnp.zeros_like(part))
         return carry
 
@@ -368,18 +416,18 @@
     at_first = lane == 0
     at_last = lane == LANES - 1
 
-    def update(j, b):
-        base = b * WIDE
+    def compute(j, b):
+        base = b * STRIP
         if not isinstance(b, int):
-            base = pl.multiple_of(base, WIDE)
+            base = pl.multiple_of(base, STRIP)
 
         def piece(k):
-            return fields_v[j, :, pl.ds(base + (k - 1) * LANES, LANES)]
+            return chain[j][:, pl.ds(base + (k - 1) * LANES, LANES)]
 
         near = [piece(k) for k in range(4)]
         back = [pltpu.roll(near[k], 1, axis=1) for k in range(3)]
         ahead = [pltpu.roll(near[k], LANES - 1, axis=1) for k in range(1, 4)]
-        here = pl.ds(base, WIDE)
+        here = pl.ds(base, STRIP)
         x = jnp.concatenate(near[1:3], axis=1)
         both = jnp.concatenate(
             [
@@ -396,13 +444,23 @@
         new = (1.0 - 2.0 * d) * x + (d * both + change)
         if j > 0:
             new = jnp.where(sub_v[:, here] > j, new, x)
+        return new
+
+    def keep(j, b, new):
+        base = b * STRIP
+        if not isinstance(b, int):
+            base = pl.multiple_of(base, STRIP)
         if j < SUBS - 1:
-            fields_v[j + 1, :, here] = new
+            chain[j + 1][:, pl.ds(base, STRIP)] = new
         else:
             there = base - LEAD
             if not isinstance(b, int):
-                there = pl.multiple_of(there, WIDE)
-            out_v[:, pl.ds(there, WIDE)] = new
+                there = pl.multiple_of(there, STRIP)
+            out_v[:, pl.ds(there, STRIP)] = new
+
+    def advance_all(i, subs):
+        for j in reversed(subs):
+            keep(j, i - 2 * j, compute(j, i - 2 * j))
 
     low_b, high_b = start - 1, start + blocks
 
@@ -417,36 +475,31 @@
     waited = 0
     last = start + blocks - 1 + 2 * (SUBS - 1)
     for i in range(low_b, body_from):
-        while waited < pieces and waited * CHUNK + start <= i + 1:
+        while waited < pieces and waited * STRIPS + start <= i + 1:
             load(waited).wait()
             waited += 1
-        for j in range(SUBS):
-            if valid(i, j):
-                update(j, i - 2 * j)
+        advance_all(i, [j for j in range(SUBS) if valid(i, j)])
 
     def body(i, carry):
         coming = i + 1 - start
 
-        @pl.when((coming % CHUNK == 0) & (coming // CHUNK >= waited) & (coming // CHUNK < pieces))
+        @pl.when((coming % STRIPS == 0) & (coming // STRIPS >= waited) & (coming // STRIPS < pieces))
         def _():
-            load(coming // CHUNK).wait()
-
-        for j in range(SUBS):
-            update(j, i - 2 * j)
+            load(coming // STRIPS).wait()
+
+        advance_all(i, list(range(SUBS)))
         ended = i - 2 * (SUBS - 1) - start + 1
 
-        @pl.when(ended % CHUNK == 0)
+        @pl.when(ended % STRIPS == 0)
         def _():
-            store(ended // CHUNK - 1).start()
+            store(ended // STRIPS - 1).start()
 
         return carry
 
     lax.fori_loop(body_from, body_to, body, 0)
     for i in range(body_to, last + 1):
-        for j in range(SUBS):
-            if valid(i, j):
-                update(j, i - 2 * j)
-    for c in range((body_to - 1 - 2 * (SUBS - 1) - start + 1) // CHUNK, pieces):
+        advance_all(i, [j for j in range(SUBS) if valid(i, j)])
+    for c in range((body_to - 1 - 2 * (SUBS - 1) - start + 1) // STRIPS, pieces):
         store(c).start()
     for c in range(pieces):
         store(c).wait()
@@ -457,9 +510,8 @@
     levels, columns = state.shape
     fields = forcing.shape[0]
     width = columns + 2 * LEAD
-    pieces = columns // (CHUNK * WIDE)
-    anywhere = pl.BlockSpec(memory_space=pl.ANY)
-    vmem = pl.BlockSpec(memory_space=pltpu.VMEM)
+    pieces = columns // (STRIPS * STRIP)
+    hbm = pl.BlockSpec(memory_space=pltpu.HBM)
     smem = pl.BlockSpec(memory_space=pltpu.SMEM)
     return pl.pallas_call(
         functools.partial(advance_kernel, comps, doms),
@@ -467,21 +519,30 @@
             jax.ShapeDtypeStruct(state.shape, F32),
             jax.ShapeDtypeStruct(forcing.shape, F32),
         ),
-        in_specs=[smem, anywhere] + [vmem] * 8,
-        out_specs=(anywhere, anywhere),
+        in_specs=[smem] + [hbm] * 9,
+        out_specs=(hbm, hbm),
         scratch_shapes=[
-            pltpu.VMEM((SUBS, levels, width), F32),
+            pltpu.VMEM((levels, width), F32),
+            pltpu.VMEM((levels, width), F32),
+            pltpu.VMEM((levels, width), F32),
+            pltpu.VMEM((levels, width), F32),
             pltpu.VMEM((levels, columns), F32),
             pltpu.VMEM((fields, width), F32),
             pltpu.VMEM((fields, columns), F32),
             pltpu.VMEM((1, width), F32),
             pltpu.VMEM((1, width), jnp.int32),
-            pltpu.VMEM((levels, WIDE), F32),
+            pltpu.VMEM((1, columns), jnp.int32),
+            pltpu.VMEM((levels, levels), F32),
+            pltpu.VMEM((fields, levels), F32),
+            pltpu.VMEM(arrived.shape, F32),
+            pltpu.VMEM(halo.shape, F32),
+            pltpu.VMEM((levels, STRIP), F32),
             pltpu.SemaphoreType.DMA((pieces,)),
             pltpu.SemaphoreType.DMA((pieces,)),
             pltpu.SemaphoreType.DMA,
+            pltpu.SemaphoreType.DMA((8,)),
         ],
-        compiler_params=pltpu.CompilerParams(vmem_limit_bytes=48 << 20),
+        compiler_params=pltpu.CompilerParams(vmem_limit_bytes=60 << 20),
         name="advance",
     )(targets, state, forcing, vertical, inject, diffuse, substeps, landmask, arrived, halo)
 
@@ -492,10 +553,10 @@
     def local(state, forcing, vertical, inject, extract, diffuse, substeps, landmask, links, weights):
         rows = [a.reshape(1, -1) for a in (diffuse, substeps, landmask)]
         arrived, targets, halo = exchange(
-            comps, doms, links, state, forcing, extract, *rows, weights
+            comps, doms, links.swapaxes(2, 3), state, forcing, extract, *rows, weights
         )
         return advance(
-            comps, doms, targets, state, forcing, vertical, inject, *rows, arrived, halo
+            comps, doms, targets, state, forcing, vertical, inject.swapaxes(1, 2), *rows, arrived, halo
         )
 
     return jax.shard_map(

time: 72.5 us -> 43.5 us (0.60)
  Pallas kernels: 61.9 us -> 42.6 us
  local copies, waits for them, and re-layouts: 9.41 us -> 0 us
    pallas_call x1, Pallas kernels: 45.2 us -> 27 us  [advance(): pl.pallas_call(functools.partial(advance_kernel, comps, doms), out_shape=...]
    unnamed x28 -> x0, local copies, waits for them, and re-layouts: 9.41 us -> none
    pallas_call x1, Pallas kernels: 16.7 us -> 15.6 us  [exchange(): pl.pallas_call(functools.partial(exchange_kernel, comps, doms), out_shape...]
where the time goes in v2:
time: 43.5 us; the launch traced here: 43.2 us
  Pallas kernels  42.6 us (98%)
  between operations  0.64 us (1%)
    pallas_call x1, Pallas kernels, advance(): pl.pallas_call(functools.partial(advance_kernel, comps, doms), out_shape=...  27 us
    pallas_call x1, Pallas kernels, exchange(): pl.pallas_call(functools.partial(exchange_kernel, comps, doms), out_shape...  15.6 us

profile of v2, /device:TPU:5, one launch (start us, length us, event | category | flops | bytes accessed | tf_op | source)
XLA Modules:
  0.0 43.2 jit_solution(7584091979106326588)
XLA Ops:
  0.6 15.6 %exchange.1 = (f32[32,16,128]{2,1,0:T(8,128)}, s32[32,1,128]{2,1,0:T(1,128)}, f32[2,96,128]{2,1,0:T(8,128)}) custom-call(s32[3,1,2,32]{3,2,1,0:T(2,128)} %bitcast.12, f32[72,16384]{1,0:T(8,128)} %state.3, f32[8,16384]{1,0:T(8,128)} %forcing.3, f32[1,8,72]{2,1,0:T(8,128)} %extract.1, f32[1,16384]{1,0:T(1,128)} %bitcast.5, s32[1,16384]{1,0:T(1,128)} %bitcast.7, ...), custom_call_target="tpu_custom_call" | custom-call | tf_op jit(solution)/shard_map/exchange/pallas_call | solution.py:258
  16.3 27.0 %advance.1 = (f32[72,16384]{1,0:T(8,128)}, f32[8,16384]{1,0:T(8,128)}) custom-call(s32[32,1,128]{2,1,0:T(1,128)} %get-tuple-element.5.targets, f32[72,16384]{1,0:T(8,128)} %state.3, f32[8,16384]{1,0:T(8,128)} %forcing.3, f32[1,72,72]{2,1,0:T(8,128)} %vertical.1, f32[1,8,72]{2,1,0:T(8,128)} %bitcast.11, f32[1,16384]{1,0:T(1,128)} %bitcast.6, ...), custom_call_target="tpu_custom_call" | custom-call | tf_op jit(solution)/shard_map/advance/pallas_call | solution.py:516

commit v3 on v2

--- a/solution.py
+++ b/solution.py
@@ -11,7 +11,7 @@
 DT = 0.25
 LANES = 128
 WIDE = 256
-STRIP = 256
+STRIP = 512
 LEAD = 2 * STRIP
 STRIPS = 2048 // STRIP
 GROUP = 8
@@ -424,18 +424,12 @@
         def piece(k):
             return chain[j][:, pl.ds(base + (k - 1) * LANES, LANES)]
 
-        near = [piece(k) for k in range(4)]
-        back = [pltpu.roll(near[k], 1, axis=1) for k in range(3)]
-        ahead = [pltpu.roll(near[k], LANES - 1, axis=1) for k in range(1, 4)]
         here = pl.ds(base, STRIP)
-        x = jnp.concatenate(near[1:3], axis=1)
-        both = jnp.concatenate(
-            [
-                jnp.where(at_first, back[k], back[k + 1]) + jnp.where(at_last, ahead[k + 1], ahead[k])
-                for k in range(2)
-            ],
-            axis=1,
-        )
+        x = chain[j][:, here]
+        near = chain[j][:, pl.ds(base - LANES, STRIP + 2 * LANES)]
+        both = (pltpu.roll(near, 1, axis=1) + pltpu.roll(near, STRIP + 2 * LANES - 1, axis=1))[
+            :, LANES : LANES + STRIP
+        ]
         high, low = high_low(jnp.concatenate([x, force_v[:, here]], axis=0))
         change = jnp.dot(
             left_b, jnp.concatenate([high, low, high], axis=0), preferred_element_type=F32
@@ -536,7 +530,7 @@
             pltpu.VMEM((fields, levels), F32),
             pltpu.VMEM(arrived.shape, F32),
             pltpu.VMEM(halo.shape, F32),
-            pltpu.VMEM((levels, STRIP), F32),
+            pltpu.VMEM((levels, WIDE), F32),
             pltpu.SemaphoreType.DMA((pieces,)),
             pltpu.SemaphoreType.DMA((pieces,)),
             pltpu.SemaphoreType.DMA,

time: 43.5 us -> 39.6 us (0.910)
  Pallas kernels: 42.6 us -> 38.7 us
    pallas_call x1, Pallas kernels: 27 us -> 23 us  [advance(): pl.pallas_call(functools.partial(advance_kernel, comps, doms), out_shape=...]
where the time goes in v3:
time: 39.6 us; the launch traced here: 39.3 us
  Pallas kernels  38.7 us (98%)
  between operations  0.64 us (2%)
    pallas_call x1, Pallas kernels, advance(): pl.pallas_call(functools.partial(advance_kernel, comps, doms), out_shape=...  23 us
    pallas_call x1, Pallas kernels, exchange(): pl.pallas_call(functools.partial(exchange_kernel, comps, doms), out_shape...  15.6 us

profile of v3, /device:TPU:5, one launch (start us, length us, event | category | flops | bytes accessed | tf_op | source)
XLA Modules:
  0.0 39.3 jit_solution(13456034899544805422)
XLA Ops:
  0.6 15.6 %exchange.1 = (f32[32,16,128]{2,1,0:T(8,128)}, s32[32,1,128]{2,1,0:T(1,128)}, f32[2,96,128]{2,1,0:T(8,128)}) custom-call(s32[3,1,2,32]{3,2,1,0:T(2,128)} %bitcast.12, f32[72,16384]{1,0:T(8,128)} %state.3, f32[8,16384]{1,0:T(8,128)} %forcing.3, f32[1,8,72]{2,1,0:T(8,128)} %extract.1, f32[1,16384]{1,0:T(1,128)} %bitcast.5, s32[1,16384]{1,0:T(1,128)} %bitcast.7, ...), custom_call_target="tpu_custom_call" | custom-call | tf_op jit(solution)/shard_map/exchange/pallas_call | solution.py:258
  16.3 23.0 %advance.1 = (f32[72,16384]{1,0:T(8,128)}, f32[8,16384]{1,0:T(8,128)}) custom-call(s32[32,1,128]{2,1,0:T(1,128)} %get-tuple-element.5.targets, f32[72,16384]{1,0:T(8,128)} %state.3, f32[8,16384]{1,0:T(8,128)} %forcing.3, f32[1,72,72]{2,1,0:T(8,128)} %vertical.1, f32[1,8,72]{2,1,0:T(8,128)} %bitcast.11, f32[1,16384]{1,0:T(1,128)} %bitcast.6, ...), custom_call_target="tpu_custom_call" | custom-call | tf_op jit(solution)/shard_map/advance/pallas_call | solution.py:510
